TPU v7x, 32 devices: a whole 2x2x4 slice. The times are simulated.
32 devices in a mesh: row: 4 (over y, x), col: 8 (over z, core).
Axes of the slice: x: 2, y: 2, z: 4, core: 2. Of those that a mesh axis runs over, the one named last changes fastest.
Arguments:
- u_field: float32 [128, 8192], P('row', 'col'), may hold values from -4 to 4
- v_field: float32 [128, 8192], P('row', 'col'), may hold values from -7.5 to 7.5
- stimulus: float32 [128, 8192], P('row', 'col'), may hold values from -6 to 6
Outputs:
- u_final: float32 [128, 8192], P('row', 'col')
- v_final: float32 [128, 8192], P('row', 'col')
All inputs are finite; a program needn't handle non-finite values.
Results may differ from a plain program's by a relative error of at most 0.0003.
Values sent between devices are 32-bit elements; how exact they have to be, the bound alone decides.
No kernel may reach another device: no remote copies, remote signals or barrier semaphores. Data moves between devices by JAX's collectives and lax.ppermute only.
A program may use at most 64 MiB of HBM per device.

v0:
```python
import jax
import jax.numpy as jnp
from jax import lax
from jax.sharding import PartitionSpec as P

MICRO_COUNT = 4
MIDDLE = 3
TOP = 3
OUTER = 2


RATE_U = 0.125
RATE_V = 0.125
TIME_STEP = 0.05
RECOVERY = 0.08
OFFSET = 0.7
DAMPING = 0.8


def extended(block, sides, width):
    for axis, dim in sides:
        count = lax.axis_size(axis)
        forward = [(i, i + 1) for i in range(count - 1)]
        forward.append((count - 1, 0))
        backward = [(target, source) for source, target in forward]
        low = lax.ppermute(
            lax.slice_in_dim(block, block.shape[dim] - width, None, axis=dim), axis, forward
        )
        high = lax.ppermute(lax.slice_in_dim(block, 0, width, axis=dim), axis, backward)
        block = jnp.concatenate([low, block, high], axis=dim)
    return block


def advance(padded, stimulus):
    centre = padded[:, 1:-1, 1:-1]
    beside_all = padded[:, :-2, 1:-1] + padded[:, 2:, 1:-1]
    beside_all = beside_all + padded[:, 1:-1, :-2] + padded[:, 1:-1, 2:]
    beside_all = beside_all - 4.0 * centre
    u_now = centre[0]
    v_now = centre[1]
    u_next = (
        u_now
        + RATE_U * beside_all[0]
        + TIME_STEP * (u_now - u_now * u_now * u_now / 3.0 - v_now + stimulus)
    )
    v_next = (
        v_now + RATE_V * beside_all[1] + TIME_STEP * RECOVERY * (u_now + OFFSET - DAMPING * v_now)
    )
    return jnp.stack([u_next, v_next])


def forward_linear_jump(inner, repeats, fields):

    def turn(present_index, pair_now):
        return (pair_now[1], inner(pair_now[1]))

    previous_fields, latest = lax.fori_loop(0, repeats, turn, (fields, fields))
    return latest + (latest - previous_fields)


def body(u_field, v_field, stimulus):
    fields = jnp.stack([u_field, v_field])
    halo_width_total = MIDDLE * MICRO_COUNT
    stim_wide = extended(stimulus, (("row", 0), ("col", 1)), halo_width_total)
    height = stim_wide.shape[0]
    breadth = stim_wide.shape[1]

    def local_first(padded, depth):
        previous_fields = padded
        for telescope_advance_once in range(MICRO_COUNT):
            if telescope_advance_once == MICRO_COUNT - 1:
                previous_fields = padded[:, 1:-1, 1:-1]
            depth = depth - 1
            inset = halo_width_total - depth
            window = stim_wide[inset : height - inset, inset : breadth - inset]
            padded = advance(padded, window)
        return padded + (padded - previous_fields)

    def second(initial_fields_pair):
        padded = extended(initial_fields_pair, (("row", 1), ("col", 2)), halo_width_total)
        previous_fields = padded
        depth = halo_width_total
        for middle_step in range(MIDDLE):
            if middle_step == MIDDLE - 1:
                previous_fields = padded[:, MICRO_COUNT:-MICRO_COUNT, MICRO_COUNT:-MICRO_COUNT]
            padded = local_first(padded, depth)
            depth = depth - MICRO_COUNT
        return padded + (padded - previous_fields)

    final_fields = lax.fori_loop(
        0,
        OUTER,
        lambda present_index, state_now: forward_linear_jump(second, TOP, state_now),
        fields,
    )
    return (final_fields[0], final_fields[1])


def solution(mesh):
    return jax.shard_map(
        body,
        mesh=mesh,
        in_specs=(P("row", "col"), P("row", "col"), P("row", "col")),
        out_specs=(P("row", "col"), P("row", "col")),
        check_vma=False,
    )
```

profile of v0, /device:TPU:0, one launch (start us, length us, event | category | flops | bytes accessed | tf_op | source)
XLA Modules:
  0.0 173.7 jit_solution(9367069396672715699)
XLA Ops:
  0.6 0.9 fusion.214
  1.6 3.0 %collective-permute-start.4 = (f32[12,1024]{1,0:T(8,128)S(1)}, f32[12,1024]{1,0:T(8,128)S(1)}, u32[]{:S(2)}, u32[]{:S(2)}) collective-permute-start(f32[12,1024]{1,0:T(8,128)S(1)} %get-tuple-element.80), channel_id=1, source_target_pairs={{0,8},{8,16},{16,24},{24,0},{1,9},{9,17},{17,25},{25,1},{2,10},{10... | collective-permute-start | bytes 147464 | tf_op jit(solution)/shard_map/ppermute | solution.py:26
  4.6 1.0 collective-permute-start.5
  5.6 2.3 %collective-permute-done.4 = f32[12,1024]{1,0:T(8,128)S(1)} collective-permute-done((f32[12,1024]{1,0:T(8,128)S(1)}, f32[12,1024]{1,0:T(8,128)S(1)}, u32[]{:S(2)}, u32[]{:S(2)}) %collective-permute-start.4) | collective-permute-done | bytes 49184 | tf_op jit(solution)/shard_map/ppermute | solution.py:26
  7.9 1.4 collective-permute-done.5
  9.4 2.2 %collective-permute-start.7 = (f32[56,12]{1,0:T(8,128)S(1)}, f32[56,12]{1,0:T(8,128)S(1)}, u32[]{:S(2)}, u32[]{:S(2)}) collective-permute-start(f32[56,12]{1,0:T(8,128)S(1)} %get-tuple-element.78), channel_id=1, source_target_pairs={{1,0},{2,1},{3,2},{4,3},{5,4},{6,5},{7,6},{0,7},{9,8},{10,9},{11,1... | collective-permute-start | bytes 8072 | tf_op jit(solution)/shard_map/ppermute | solution.py:29
  13.1 3.5 %collective-permute-done.6 = f32[56,12]{1,0:T(8,128)S(1)} collective-permute-done((f32[56,12]{1,0:T(8,128)S(1)}, f32[56,12]{1,0:T(8,128)S(1)}, u32[]{:S(2)}, u32[]{:S(2)}) %collective-permute-start.6) | collective-permute-done | bytes 2720 | tf_op jit(solution)/shard_map/ppermute | solution.py:26
  16.9 155.1 %while.23 = (s32[]{:T(128)}, f32[2,32,1024]{2,1,0:T(8,128)}, f32[56,1048]{1,0:T(8,128)S(1)}, f32[32,1024]{1,0:T(8,128)S(1)}, s32[]{:T(128)}, /*index=5*/s32[]{:T(128)}, s32[]{:T(128)}, f32[32,1024]{1,0:T(8,128)}) while((s32[]{:T(128)}, f32[2,32,1024]{2,1,0:T(8,128)}, f32[56,1048]{1,0:T(8,128)S(1)}, f32[32,1024]{1,0:T(8,128)S(1)}, s32[]{:T(128)}, ...), condition=%wide.region_3.0_spmd, body=%wide.region_0.0_spmd.sunk | while | flops 19830928 | bytes 40506832 | solution.py:90
  16.9 1.0 copy.7
  17.8 75.2 %while.24 = (s32[]{:T(128)}, f32[2,32,1024]{2,1,0:T(8,128)}, f32[2,32,1024]{2,1,0:T(8,128)S(1)}, f32[56,1048]{1,0:T(8,128)S(1)}, f32[32,1024]{1,0:T(8,128)S(1)}, /*index=5*/s32[]{:T(128)}) while((s32[]{:T(128)}, f32[2,32,1024]{2,1,0:T(8,128)}, f32[2,32,1024]{2,1,0:T(8,128)S(1)}, f32[56,1048]{1,0:T(8,128)S(1)}, f32[32,1024]{1,0:T(8,128)S(1)}, ...), condition=%wide.region_2.0_spmd, body=%wide.region_1.0_spmd.sunk | while | flops 19699856 | bytes 39195972 | solution.py:57
  17.8 2.1 %collective-permute-start = (f32[2,12,1024]{2,1,0:T(8,128)S(1)}, f32[2,12,1024]{2,1,0:T(8,128)S(1)}, u32[]{:S(2)}, u32[]{:S(2)}) collective-permute-start(f32[2,12,1024]{2,1,0:T(8,128)S(1)} %get-tuple-element.157), channel_id=1, source_target_pairs={{8,0},{16,8},{24,16},{0,24},{9,1},{17,9},{25,17},{1,25},{10,2},{18... | collective-permute-start | bytes 294920 | tf_op jit(solution)/shard_map/while/body/eval_jaxpr/while/body/eval_jaxpr/ppermute | solution.py:29
  20.0 2.9 %collective-permute-done = f32[2,12,1024]{2,1,0:T(8,128)S(1)} collective-permute-done((f32[2,12,1024]{2,1,0:T(8,128)S(1)}, f32[2,12,1024]{2,1,0:T(8,128)S(1)}, u32[]{:S(2)}, u32[]{:S(2)}) %collective-permute-start) | collective-permute-done | bytes 98336 | tf_op jit(solution)/shard_map/while/body/eval_jaxpr/while/body/eval_jaxpr/ppermute | solution.py:29
  22.9 2.9 %collective-permute-done.1 = f32[2,12,1024]{2,1,0:T(8,128)S(1)} collective-permute-done((f32[2,12,1024]{2,1,0:T(8,128)S(1)}, f32[2,12,1024]{2,1,0:T(8,128)S(1)}, u32[]{:S(2)}, u32[]{:S(2)}) %collective-permute-start.1) | collective-permute-done | bytes 98336 | tf_op jit(solution)/shard_map/while/body/eval_jaxpr/while/body/eval_jaxpr/ppermute | solution.py:26
  25.9 3.5 %collective-permute-start.3 = (f32[2,56,12]{2,1,0:T(8,128)S(1)}, f32[2,56,12]{2,1,0:T(8,128)S(1)}, u32[]{:S(2)}, u32[]{:S(2)}) collective-permute-start(f32[2,56,12]{2,1,0:T(8,128)S(1)} %get-tuple-element.160), channel_id=1, source_target_pairs={{1,0},{2,1},{3,2},{4,3},{5,4},{6,5},{7,6},{0,7},{9,8},{10,9},{11,1... | collective-permute-start | bytes 16136 | tf_op jit(solution)/shard_map/while/body/eval_jaxpr/while/body/eval_jaxpr/ppermute | solution.py:29
  30.1 1.7 %collective-permute-done.2 = f32[2,56,12]{2,1,0:T(8,128)S(1)} collective-permute-done((f32[2,56,12]{2,1,0:T(8,128)S(1)}, f32[2,56,12]{2,1,0:T(8,128)S(1)}, u32[]{:S(2)}, u32[]{:S(2)}) %collective-permute-start.2) | collective-permute-done | bytes 5408 | tf_op jit(solution)/shard_map/while/body/eval_jaxpr/while/body/eval_jaxpr/ppermute | solution.py:26
  44.0 0.9 collective-permute-start
  44.9 1.1 collective-permute-start.1
  46.0 2.9 %collective-permute-done = f32[2,12,1024]{2,1,0:T(8,128)S(1)} collective-permute-done((f32[2,12,1024]{2,1,0:T(8,128)S(1)}, f32[2,12,1024]{2,1,0:T(8,128)S(1)}, u32[]{:S(2)}, u32[]{:S(2)}) %collective-permute-start) | collective-permute-done | bytes 98336 | tf_op jit(solution)/shard_map/while/body/eval_jaxpr/while/body/eval_jaxpr/ppermute | solution.py:29
  49.0 1.8 %collective-permute-done.1 = f32[2,12,1024]{2,1,0:T(8,128)S(1)} collective-permute-done((f32[2,12,1024]{2,1,0:T(8,128)S(1)}, f32[2,12,1024]{2,1,0:T(8,128)S(1)}, u32[]{:S(2)}, u32[]{:S(2)}) %collective-permute-start.1) | collective-permute-done | bytes 98336 | tf_op jit(solution)/shard_map/while/body/eval_jaxpr/while/body/eval_jaxpr/ppermute | solution.py:26
  51.0 3.5 %collective-permute-start.3 = (f32[2,56,12]{2,1,0:T(8,128)S(1)}, f32[2,56,12]{2,1,0:T(8,128)S(1)}, u32[]{:S(2)}, u32[]{:S(2)}) collective-permute-start(f32[2,56,12]{2,1,0:T(8,128)S(1)} %get-tuple-element.160), channel_id=1, source_target_pairs={{1,0},{2,1},{3,2},{4,3},{5,4},{6,5},{7,6},{0,7},{9,8},{10,9},{11,1... | collective-permute-start | bytes 16136 | tf_op jit(solution)/shard_map/while/body/eval_jaxpr/while/body/eval_jaxpr/ppermute | solution.py:29
  55.2 1.6 collective-permute-done.2
  69.3 1.6 collective-permute-start.1
  70.9 2.9 %collective-permute-done = f32[2,12,1024]{2,1,0:T(8,128)S(1)} collective-permute-done((f32[2,12,1024]{2,1,0:T(8,128)S(1)}, f32[2,12,1024]{2,1,0:T(8,128)S(1)}, u32[]{:S(2)}, u32[]{:S(2)}) %collective-permute-start) | collective-permute-done | bytes 98336 | tf_op jit(solution)/shard_map/while/body/eval_jaxpr/while/body/eval_jaxpr/ppermute | solution.py:29
  73.9 1.5 collective-permute-done.1
  75.5 3.5 %collective-permute-start.3 = (f32[2,56,12]{2,1,0:T(8,128)S(1)}, f32[2,56,12]{2,1,0:T(8,128)S(1)}, u32[]{:S(2)}, u32[]{:S(2)}) collective-permute-start(f32[2,56,12]{2,1,0:T(8,128)S(1)} %get-tuple-element.160), channel_id=1, source_target_pairs={{1,0},{2,1},{3,2},{4,3},{5,4},{6,5},{7,6},{0,7},{9,8},{10,9},{11,1... | collective-permute-start | bytes 16136 | tf_op jit(solution)/shard_map/while/body/eval_jaxpr/while/body/eval_jaxpr/ppermute | solution.py:29
  79.7 1.3 collective-permute-done.2
  93.1 1.7 subtract_add_fusion.9
  94.8 0.9 copy.7
  95.7 74.6 %while.24 = (s32[]{:T(128)}, f32[2,32,1024]{2,1,0:T(8,128)}, f32[2,32,1024]{2,1,0:T(8,128)S(1)}, f32[56,1048]{1,0:T(8,128)S(1)}, f32[32,1024]{1,0:T(8,128)S(1)}, /*index=5*/s32[]{:T(128)}) while((s32[]{:T(128)}, f32[2,32,1024]{2,1,0:T(8,128)}, f32[2,32,1024]{2,1,0:T(8,128)S(1)}, f32[56,1048]{1,0:T(8,128)S(1)}, f32[32,1024]{1,0:T(8,128)S(1)}, ...), condition=%wide.region_2.0_spmd, body=%wide.region_1.0_spmd.sunk | while | flops 19699856 | bytes 39195972 | solution.py:57
  95.7 1.2 collective-permute-start
  97.0 0.9 collective-permute-start.1
  97.8 2.9 %collective-permute-done = f32[2,12,1024]{2,1,0:T(8,128)S(1)} collective-permute-done((f32[2,12,1024]{2,1,0:T(8,128)S(1)}, f32[2,12,1024]{2,1,0:T(8,128)S(1)}, u32[]{:S(2)}, u32[]{:S(2)}) %collective-permute-start) | collective-permute-done | bytes 98336 | tf_op jit(solution)/shard_map/while/body/eval_jaxpr/while/body/eval_jaxpr/ppermute | solution.py:29
  100.7 2.3 %collective-permute-done.1 = f32[2,12,1024]{2,1,0:T(8,128)S(1)} collective-permute-done((f32[2,12,1024]{2,1,0:T(8,128)S(1)}, f32[2,12,1024]{2,1,0:T(8,128)S(1)}, u32[]{:S(2)}, u32[]{:S(2)}) %collective-permute-start.1) | collective-permute-done | bytes 98336 | tf_op jit(solution)/shard_map/while/body/eval_jaxpr/while/body/eval_jaxpr/ppermute | solution.py:26
  103.2 3.5 %collective-permute-start.3 = (f32[2,56,12]{2,1,0:T(8,128)S(1)}, f32[2,56,12]{2,1,0:T(8,128)S(1)}, u32[]{:S(2)}, u32[]{:S(2)}) collective-permute-start(f32[2,56,12]{2,1,0:T(8,128)S(1)} %get-tuple-element.160), channel_id=1, source_target_pairs={{1,0},{2,1},{3,2},{4,3},{5,4},{6,5},{7,6},{0,7},{9,8},{10,9},{11,1... | collective-permute-start | bytes 16136 | tf_op jit(solution)/shard_map/while/body/eval_jaxpr/while/body/eval_jaxpr/ppermute | solution.py:29
  107.4 1.2 collective-permute-done.2
  120.7 0.9 collective-permute-start
  121.6 1.2 collective-permute-start.1
  122.7 3.2 %collective-permute-done = f32[2,12,1024]{2,1,0:T(8,128)S(1)} collective-permute-done((f32[2,12,1024]{2,1,0:T(8,128)S(1)}, f32[2,12,1024]{2,1,0:T(8,128)S(1)}, u32[]{:S(2)}, u32[]{:S(2)}) %collective-permute-start) | collective-permute-done | bytes 98336 | tf_op jit(solution)/shard_map/while/body/eval_jaxpr/while/body/eval_jaxpr/ppermute | solution.py:29
  125.9 1.5 collective-permute-done.1
  127.6 3.5 %collective-permute-start.3 = (f32[2,56,12]{2,1,0:T(8,128)S(1)}, f32[2,56,12]{2,1,0:T(8,128)S(1)}, u32[]{:S(2)}, u32[]{:S(2)}) collective-permute-start(f32[2,56,12]{2,1,0:T(8,128)S(1)} %get-tuple-element.160), channel_id=1, source_target_pairs={{1,0},{2,1},{3,2},{4,3},{5,4},{6,5},{7,6},{0,7},{9,8},{10,9},{11,1... | collective-permute-start | bytes 16136 | tf_op jit(solution)/shard_map/while/body/eval_jaxpr/while/body/eval_jaxpr/ppermute | solution.py:29
  131.8 1.2 collective-permute-done.2
  145.1 1.6 collective-permute-start
  147.1 3.0 %collective-permute-done = f32[2,12,1024]{2,1,0:T(8,128)S(1)} collective-permute-done((f32[2,12,1024]{2,1,0:T(8,128)S(1)}, f32[2,12,1024]{2,1,0:T(8,128)S(1)}, u32[]{:S(2)}, u32[]{:S(2)}) %collective-permute-start) | collective-permute-done | bytes 98336 | tf_op jit(solution)/shard_map/while/body/eval_jaxpr/while/body/eval_jaxpr/ppermute | solution.py:29
  150.1 2.6 %collective-permute-done.1 = f32[2,12,1024]{2,1,0:T(8,128)S(1)} collective-permute-done((f32[2,12,1024]{2,1,0:T(8,128)S(1)}, f32[2,12,1024]{2,1,0:T(8,128)S(1)}, u32[]{:S(2)}, u32[]{:S(2)}) %collective-permute-start.1) | collective-permute-done | bytes 98336 | tf_op jit(solution)/shard_map/while/body/eval_jaxpr/while/body/eval_jaxpr/ppermute | solution.py:26
  152.9 3.5 %collective-permute-start.3 = (f32[2,56,12]{2,1,0:T(8,128)S(1)}, f32[2,56,12]{2,1,0:T(8,128)S(1)}, u32[]{:S(2)}, u32[]{:S(2)}) collective-permute-start(f32[2,56,12]{2,1,0:T(8,128)S(1)} %get-tuple-element.160), channel_id=1, source_target_pairs={{1,0},{2,1},{3,2},{4,3},{5,4},{6,5},{7,6},{0,7},{9,8},{10,9},{11,1... | collective-permute-start | bytes 16136 | tf_op jit(solution)/shard_map/while/body/eval_jaxpr/while/body/eval_jaxpr/ppermute | solution.py:29
  157.1 1.2 collective-permute-done.2
  170.3 1.7 subtract_add_fusion.9
  172.0 1.7 slice_bitcast_fusion
  (287 shorter events, 78.9 us)
Async XLA Ops:
  0.6 8.7 %copy-start = (f32[32,1024]{1,0:T(8,128)S(1)}, f32[32,1024]{1,0:T(8,128)}, u32[]{:S(2)}) copy-start(f32[32,1024]{1,0:T(8,128)} %param.9) | copy-start | bytes 393220
  1.6 6.3 %collective-permute-start.4 = (f32[12,1024]{1,0:T(8,128)S(1)}, f32[12,1024]{1,0:T(8,128)S(1)}, u32[]{:S(2)}, u32[]{:S(2)}) collective-permute-start(f32[12,1024]{1,0:T(8,128)S(1)} %get-tuple-element.80), channel_id=1, source_target_pairs={{0,8},{8,16},{16,24},{24,0},{1,9},{9,17},{17,25},{25,1},{2,10},{10... | collective-permute-start | bytes 147464 | tf_op jit(solution)/shard_map/ppermute | solution.py:26
  4.6 4.7 %collective-permute-start.5 = (f32[12,1024]{1,0:T(8,128)S(1)}, f32[12,1024]{1,0:T(8,128)S(1)}, u32[]{:S(2)}, u32[]{:S(2)}) collective-permute-start(f32[12,1024]{1,0:T(8,128)S(1)} %get-tuple-element.81), channel_id=1, source_target_pairs={{8,0},{16,8},{24,16},{0,24},{9,1},{17,9},{25,17},{1,25},{10,2},{18... | collective-permute-start | bytes 147464 | tf_op jit(solution)/shard_map/ppermute | solution.py:29
  9.3 2.3 %copy-start.2 = (f32[32,1024]{1,0:T(8,128)S(1)}, f32[32,1024]{1,0:T(8,128)}, u32[]{:S(2)}) copy-start(f32[32,1024]{1,0:T(8,128)} %param.8) | copy-start | bytes 393220
  9.3 2.3 %copy-start.3 = (f32[32,1024]{1,0:T(8,128)S(1)}, f32[32,1024]{1,0:T(8,128)}, u32[]{:S(2)}) copy-start(f32[32,1024]{1,0:T(8,128)} %param.7) | copy-start | bytes 393220
  9.4 3.8 %collective-permute-start.7 = (f32[56,12]{1,0:T(8,128)S(1)}, f32[56,12]{1,0:T(8,128)S(1)}, u32[]{:S(2)}, u32[]{:S(2)}) collective-permute-start(f32[56,12]{1,0:T(8,128)S(1)} %get-tuple-element.78), channel_id=1, source_target_pairs={{1,0},{2,1},{3,2},{4,3},{5,4},{6,5},{7,6},{0,7},{9,8},{10,9},{11,1... | collective-permute-start | bytes 8072 | tf_op jit(solution)/shard_map/ppermute | solution.py:29
  11.6 5.1 %collective-permute-start.6 = (f32[56,12]{1,0:T(8,128)S(1)}, f32[56,12]{1,0:T(8,128)S(1)}, u32[]{:S(2)}, u32[]{:S(2)}) collective-permute-start(f32[56,12]{1,0:T(8,128)S(1)} %get-tuple-element.79), channel_id=1, source_target_pairs={{0,1},{1,2},{2,3},{3,4},{4,5},{5,6},{6,7},{7,0},{8,9},{9,10},{10,1... | collective-permute-start | bytes 8072 | tf_op jit(solution)/shard_map/ppermute | solution.py:26
  12.3 4.5 %copy-start.1 = (f32[32,1024]{1,0:T(8,128)S(1)}, f32[32,1024]{1,0:T(8,128)}, u32[]{:S(2)}) copy-start(f32[32,1024]{1,0:T(8,128)} %param.9) | copy-start | bytes 393220
  17.8 5.1 %collective-permute-start = (f32[2,12,1024]{2,1,0:T(8,128)S(1)}, f32[2,12,1024]{2,1,0:T(8,128)S(1)}, u32[]{:S(2)}, u32[]{:S(2)}) collective-permute-start(f32[2,12,1024]{2,1,0:T(8,128)S(1)} %get-tuple-element.157), channel_id=1, source_target_pairs={{8,0},{16,8},{24,16},{0,24},{9,1},{17,9},{25,17},{1,25},{10,2},{18... | collective-permute-start | bytes 294920 | tf_op jit(solution)/shard_map/while/body/eval_jaxpr/while/body/eval_jaxpr/ppermute | solution.py:29
  19.9 5.9 %collective-permute-start.1 = (f32[2,12,1024]{2,1,0:T(8,128)S(1)}, f32[2,12,1024]{2,1,0:T(8,128)S(1)}, u32[]{:S(2)}, u32[]{:S(2)}) collective-permute-start(f32[2,12,1024]{2,1,0:T(8,128)S(1)} %get-tuple-element.158), channel_id=1, source_target_pairs={{0,8},{8,16},{16,24},{24,0},{1,9},{9,17},{17,25},{25,1},{2,10},{10... | collective-permute-start | bytes 294920 | tf_op jit(solution)/shard_map/while/body/eval_jaxpr/while/body/eval_jaxpr/ppermute | solution.py:26
  25.9 6.0 %collective-permute-start.2 = (f32[2,56,12]{2,1,0:T(8,128)S(1)}, f32[2,56,12]{2,1,0:T(8,128)S(1)}, u32[]{:S(2)}, u32[]{:S(2)}) collective-permute-start(f32[2,56,12]{2,1,0:T(8,128)S(1)} %get-tuple-element.159), channel_id=1, source_target_pairs={{0,1},{1,2},{2,3},{3,4},{4,5},{5,6},{6,7},{7,0},{8,9},{9,10},{10,1... | collective-permute-start | bytes 16136 | tf_op jit(solution)/shard_map/while/body/eval_jaxpr/while/body/eval_jaxpr/ppermute | solution.py:26
  25.9 6.0 %collective-permute-start.3 = (f32[2,56,12]{2,1,0:T(8,128)S(1)}, f32[2,56,12]{2,1,0:T(8,128)S(1)}, u32[]{:S(2)}, u32[]{:S(2)}) collective-permute-start(f32[2,56,12]{2,1,0:T(8,128)S(1)} %get-tuple-element.160), channel_id=1, source_target_pairs={{1,0},{2,1},{3,2},{4,3},{5,4},{6,5},{7,6},{0,7},{9,8},{10,9},{11,1... | collective-permute-start | bytes 16136 | tf_op jit(solution)/shard_map/while/body/eval_jaxpr/while/body/eval_jaxpr/ppermute | solution.py:29
  44.0 5.0 %collective-permute-start = (f32[2,12,1024]{2,1,0:T(8,128)S(1)}, f32[2,12,1024]{2,1,0:T(8,128)S(1)}, u32[]{:S(2)}, u32[]{:S(2)}) collective-permute-start(f32[2,12,1024]{2,1,0:T(8,128)S(1)} %get-tuple-element.157), channel_id=1, source_target_pairs={{8,0},{16,8},{24,16},{0,24},{9,1},{17,9},{25,17},{1,25},{10,2},{18... | collective-permute-start | bytes 294920 | tf_op jit(solution)/shard_map/while/body/eval_jaxpr/while/body/eval_jaxpr/ppermute | solution.py:29
  44.9 5.9 %collective-permute-start.1 = (f32[2,12,1024]{2,1,0:T(8,128)S(1)}, f32[2,12,1024]{2,1,0:T(8,128)S(1)}, u32[]{:S(2)}, u32[]{:S(2)}) collective-permute-start(f32[2,12,1024]{2,1,0:T(8,128)S(1)} %get-tuple-element.158), channel_id=1, source_target_pairs={{0,8},{8,16},{16,24},{24,0},{1,9},{9,17},{17,25},{25,1},{2,10},{10... | collective-permute-start | bytes 294920 | tf_op jit(solution)/shard_map/while/body/eval_jaxpr/while/body/eval_jaxpr/ppermute | solution.py:26
  50.9 5.8 %collective-permute-start.2 = (f32[2,56,12]{2,1,0:T(8,128)S(1)}, f32[2,56,12]{2,1,0:T(8,128)S(1)}, u32[]{:S(2)}, u32[]{:S(2)}) collective-permute-start(f32[2,56,12]{2,1,0:T(8,128)S(1)} %get-tuple-element.159), channel_id=1, source_target_pairs={{0,1},{1,2},{2,3},{3,4},{4,5},{5,6},{6,7},{7,0},{8,9},{9,10},{10,1... | collective-permute-start | bytes 16136 | tf_op jit(solution)/shard_map/while/body/eval_jaxpr/while/body/eval_jaxpr/ppermute | solution.py:26
  51.0 5.8 %collective-permute-start.3 = (f32[2,56,12]{2,1,0:T(8,128)S(1)}, f32[2,56,12]{2,1,0:T(8,128)S(1)}, u32[]{:S(2)}, u32[]{:S(2)}) collective-permute-start(f32[2,56,12]{2,1,0:T(8,128)S(1)} %get-tuple-element.160), channel_id=1, source_target_pairs={{1,0},{2,1},{3,2},{4,3},{5,4},{6,5},{7,6},{0,7},{9,8},{10,9},{11,1... | collective-permute-start | bytes 16136 | tf_op jit(solution)/shard_map/while/body/eval_jaxpr/while/body/eval_jaxpr/ppermute | solution.py:29
  68.8 5.0 %collective-permute-start = (f32[2,12,1024]{2,1,0:T(8,128)S(1)}, f32[2,12,1024]{2,1,0:T(8,128)S(1)}, u32[]{:S(2)}, u32[]{:S(2)}) collective-permute-start(f32[2,12,1024]{2,1,0:T(8,128)S(1)} %get-tuple-element.157), channel_id=1, source_target_pairs={{8,0},{16,8},{24,16},{0,24},{9,1},{17,9},{25,17},{1,25},{10,2},{18... | collective-permute-start | bytes 294920 | tf_op jit(solution)/shard_map/while/body/eval_jaxpr/while/body/eval_jaxpr/ppermute | solution.py:29
  69.3 6.0 %collective-permute-start.1 = (f32[2,12,1024]{2,1,0:T(8,128)S(1)}, f32[2,12,1024]{2,1,0:T(8,128)S(1)}, u32[]{:S(2)}, u32[]{:S(2)}) collective-permute-start(f32[2,12,1024]{2,1,0:T(8,128)S(1)} %get-tuple-element.158), channel_id=1, source_target_pairs={{0,8},{8,16},{16,24},{24,0},{1,9},{9,17},{17,25},{25,1},{2,10},{10... | collective-permute-start | bytes 294920 | tf_op jit(solution)/shard_map/while/body/eval_jaxpr/while/body/eval_jaxpr/ppermute | solution.py:26
  75.5 5.6 %collective-permute-start.2 = (f32[2,56,12]{2,1,0:T(8,128)S(1)}, f32[2,56,12]{2,1,0:T(8,128)S(1)}, u32[]{:S(2)}, u32[]{:S(2)}) collective-permute-start(f32[2,56,12]{2,1,0:T(8,128)S(1)} %get-tuple-element.159), channel_id=1, source_target_pairs={{0,1},{1,2},{2,3},{3,4},{4,5},{5,6},{6,7},{7,0},{8,9},{9,10},{10,1... | collective-permute-start | bytes 16136 | tf_op jit(solution)/shard_map/while/body/eval_jaxpr/while/body/eval_jaxpr/ppermute | solution.py:26
  75.5 5.6 %collective-permute-start.3 = (f32[2,56,12]{2,1,0:T(8,128)S(1)}, f32[2,56,12]{2,1,0:T(8,128)S(1)}, u32[]{:S(2)}, u32[]{:S(2)}) collective-permute-start(f32[2,56,12]{2,1,0:T(8,128)S(1)} %get-tuple-element.160), channel_id=1, source_target_pairs={{1,0},{2,1},{3,2},{4,3},{5,4},{6,5},{7,6},{0,7},{9,8},{10,9},{11,1... | collective-permute-start | bytes 16136 | tf_op jit(solution)/shard_map/while/body/eval_jaxpr/while/body/eval_jaxpr/ppermute | solution.py:29
  95.7 5.0 %collective-permute-start = (f32[2,12,1024]{2,1,0:T(8,128)S(1)}, f32[2,12,1024]{2,1,0:T(8,128)S(1)}, u32[]{:S(2)}, u32[]{:S(2)}) collective-permute-start(f32[2,12,1024]{2,1,0:T(8,128)S(1)} %get-tuple-element.157), channel_id=1, source_target_pairs={{8,0},{16,8},{24,16},{0,24},{9,1},{17,9},{25,17},{1,25},{10,2},{18... | collective-permute-start | bytes 294920 | tf_op jit(solution)/shard_map/while/body/eval_jaxpr/while/body/eval_jaxpr/ppermute | solution.py:29
  97.0 6.1 %collective-permute-start.1 = (f32[2,12,1024]{2,1,0:T(8,128)S(1)}, f32[2,12,1024]{2,1,0:T(8,128)S(1)}, u32[]{:S(2)}, u32[]{:S(2)}) collective-permute-start(f32[2,12,1024]{2,1,0:T(8,128)S(1)} %get-tuple-element.158), channel_id=1, source_target_pairs={{0,8},{8,16},{16,24},{24,0},{1,9},{9,17},{17,25},{25,1},{2,10},{10... | collective-permute-start | bytes 294920 | tf_op jit(solution)/shard_map/while/body/eval_jaxpr/while/body/eval_jaxpr/ppermute | solution.py:26
  103.2 5.4 %collective-permute-start.2 = (f32[2,56,12]{2,1,0:T(8,128)S(1)}, f32[2,56,12]{2,1,0:T(8,128)S(1)}, u32[]{:S(2)}, u32[]{:S(2)}) collective-permute-start(f32[2,56,12]{2,1,0:T(8,128)S(1)} %get-tuple-element.159), channel_id=1, source_target_pairs={{0,1},{1,2},{2,3},{3,4},{4,5},{5,6},{6,7},{7,0},{8,9},{9,10},{10,1... | collective-permute-start | bytes 16136 | tf_op jit(solution)/shard_map/while/body/eval_jaxpr/while/body/eval_jaxpr/ppermute | solution.py:26
  103.2 5.4 %collective-permute-start.3 = (f32[2,56,12]{2,1,0:T(8,128)S(1)}, f32[2,56,12]{2,1,0:T(8,128)S(1)}, u32[]{:S(2)}, u32[]{:S(2)}) collective-permute-start(f32[2,56,12]{2,1,0:T(8,128)S(1)} %get-tuple-element.160), channel_id=1, source_target_pairs={{1,0},{2,1},{3,2},{4,3},{5,4},{6,5},{7,6},{0,7},{9,8},{10,9},{11,1... | collective-permute-start | bytes 16136 | tf_op jit(solution)/shard_map/while/body/eval_jaxpr/while/body/eval_jaxpr/ppermute | solution.py:29
  120.7 5.2 %collective-permute-start = (f32[2,12,1024]{2,1,0:T(8,128)S(1)}, f32[2,12,1024]{2,1,0:T(8,128)S(1)}, u32[]{:S(2)}, u32[]{:S(2)}) collective-permute-start(f32[2,12,1024]{2,1,0:T(8,128)S(1)} %get-tuple-element.157), channel_id=1, source_target_pairs={{8,0},{16,8},{24,16},{0,24},{9,1},{17,9},{25,17},{1,25},{10,2},{18... | collective-permute-start | bytes 294920 | tf_op jit(solution)/shard_map/while/body/eval_jaxpr/while/body/eval_jaxpr/ppermute | solution.py:29
  121.6 5.9 %collective-permute-start.1 = (f32[2,12,1024]{2,1,0:T(8,128)S(1)}, f32[2,12,1024]{2,1,0:T(8,128)S(1)}, u32[]{:S(2)}, u32[]{:S(2)}) collective-permute-start(f32[2,12,1024]{2,1,0:T(8,128)S(1)} %get-tuple-element.158), channel_id=1, source_target_pairs={{0,8},{8,16},{16,24},{24,0},{1,9},{9,17},{17,25},{25,1},{2,10},{10... | collective-permute-start | bytes 294920 | tf_op jit(solution)/shard_map/while/body/eval_jaxpr/while/body/eval_jaxpr/ppermute | solution.py:26
  127.6 5.4 %collective-permute-start.2 = (f32[2,56,12]{2,1,0:T(8,128)S(1)}, f32[2,56,12]{2,1,0:T(8,128)S(1)}, u32[]{:S(2)}, u32[]{:S(2)}) collective-permute-start(f32[2,56,12]{2,1,0:T(8,128)S(1)} %get-tuple-element.159), channel_id=1, source_target_pairs={{0,1},{1,2},{2,3},{3,4},{4,5},{5,6},{6,7},{7,0},{8,9},{9,10},{10,1... | collective-permute-start | bytes 16136 | tf_op jit(solution)/shard_map/while/body/eval_jaxpr/while/body/eval_jaxpr/ppermute | solution.py:26
  127.6 5.4 %collective-permute-start.3 = (f32[2,56,12]{2,1,0:T(8,128)S(1)}, f32[2,56,12]{2,1,0:T(8,128)S(1)}, u32[]{:S(2)}, u32[]{:S(2)}) collective-permute-start(f32[2,56,12]{2,1,0:T(8,128)S(1)} %get-tuple-element.160), channel_id=1, source_target_pairs={{1,0},{2,1},{3,2},{4,3},{5,4},{6,5},{7,6},{0,7},{9,8},{10,9},{11,1... | collective-permute-start | bytes 16136 | tf_op jit(solution)/shard_map/while/body/eval_jaxpr/while/body/eval_jaxpr/ppermute | solution.py:29
  145.1 5.1 %collective-permute-start = (f32[2,12,1024]{2,1,0:T(8,128)S(1)}, f32[2,12,1024]{2,1,0:T(8,128)S(1)}, u32[]{:S(2)}, u32[]{:S(2)}) collective-permute-start(f32[2,12,1024]{2,1,0:T(8,128)S(1)} %get-tuple-element.157), channel_id=1, source_target_pairs={{8,0},{16,8},{24,16},{0,24},{9,1},{17,9},{25,17},{1,25},{10,2},{18... | collective-permute-start | bytes 294920 | tf_op jit(solution)/shard_map/while/body/eval_jaxpr/while/body/eval_jaxpr/ppermute | solution.py:29
  146.7 6.1 %collective-permute-start.1 = (f32[2,12,1024]{2,1,0:T(8,128)S(1)}, f32[2,12,1024]{2,1,0:T(8,128)S(1)}, u32[]{:S(2)}, u32[]{:S(2)}) collective-permute-start(f32[2,12,1024]{2,1,0:T(8,128)S(1)} %get-tuple-element.158), channel_id=1, source_target_pairs={{0,8},{8,16},{16,24},{24,0},{1,9},{9,17},{17,25},{25,1},{2,10},{10... | collective-permute-start | bytes 294920 | tf_op jit(solution)/shard_map/while/body/eval_jaxpr/while/body/eval_jaxpr/ppermute | solution.py:26
  152.8 5.4 %collective-permute-start.2 = (f32[2,56,12]{2,1,0:T(8,128)S(1)}, f32[2,56,12]{2,1,0:T(8,128)S(1)}, u32[]{:S(2)}, u32[]{:S(2)}) collective-permute-start(f32[2,56,12]{2,1,0:T(8,128)S(1)} %get-tuple-element.159), channel_id=1, source_target_pairs={{0,1},{1,2},{2,3},{3,4},{4,5},{5,6},{6,7},{7,0},{8,9},{9,10},{10,1... | collective-permute-start | bytes 16136 | tf_op jit(solution)/shard_map/while/body/eval_jaxpr/while/body/eval_jaxpr/ppermute | solution.py:26
  152.9 5.4 %collective-permute-start.3 = (f32[2,56,12]{2,1,0:T(8,128)S(1)}, f32[2,56,12]{2,1,0:T(8,128)S(1)}, u32[]{:S(2)}, u32[]{:S(2)}) collective-permute-start(f32[2,56,12]{2,1,0:T(8,128)S(1)} %get-tuple-element.160), channel_id=1, source_target_pairs={{1,0},{2,1},{3,2},{4,3},{5,4},{6,5},{7,6},{0,7},{9,8},{10,9},{11,1... | collective-permute-start | bytes 16136 | tf_op jit(solution)/shard_map/while/body/eval_jaxpr/while/body/eval_jaxpr/ppermute | solution.py:29
where the time goes:
time: 174 us
  other arithmetic  73.5 us (42%)
  waiting for transfers between devices  46.6 us (27%)
  starting transfers between devices  40.1 us (23%)
  local copies, waits for them, and re-layouts  11.3 us (6%)
    sub x72, other arithmetic, advance(): beside_all = beside_all - 4.0 * centre  36.3 us
    ppermute x14, starting transfers between devices, extended(): lax.ppermute(lax.slice_in_dim(block, 0, width, axis=dim), axis, backward)  31.7 us
    ppermute x14, waiting for transfers between devices, extended(): lax.ppermute(lax.slice_in_dim(block, block.shape[dim] - width, None, axis...  26.5 us
    ppermute x14, waiting for transfers between devices, extended(): lax.ppermute(lax.slice_in_dim(block, 0, width, axis=dim), axis, backward)  20.1 us
    another operation x66, other arithmetic, advance(): return jnp.stack([u_next, v_next])  16.2 us
    add x66, other arithmetic, advance(): v_now + RATE_V * beside_all[1]  12.3 us
    ppermute x14, starting transfers between devices, extended(): lax.ppermute(lax.slice_in_dim(block, block.shape[dim] - width, None, axis...  8.4 us
    while x8, local copies, waits for them, and re-layouts  6.04 us
  transfers between devices with their start and end apart: 28, of which 22 were waited for; matrix products, arithmetic and copies ran while one was open for 3% of the time, Pallas kernels for 0%

commit v1 on v0

v1 whole, which is shorter than its diff:
```python
import functools

import jax
import jax.numpy as jnp
from jax import lax
from jax.experimental import pallas as pl
from jax.experimental.pallas import tpu as pltpu
from jax.sharding import PartitionSpec as P

MICRO_COUNT = 4
MIDDLE = 3
TOP = 3
OUTER = 2

RATE = 0.125
TIME_STEP = 0.05
RECOVERY = 0.08
OFFSET = 0.7
DAMPING = 0.8

CENTRE = OFFSET / DAMPING
UNIT_U = (3.0 * RATE / TIME_STEP) ** 0.5
UNIT_V = UNIT_U * RATE / TIME_STEP
KEEP_U = (1.0 - 4.0 * RATE + TIME_STEP) / RATE
KEEP_V = (1.0 - 4.0 * RATE - TIME_STEP * RECOVERY * DAMPING) / RATE
FEED = TIME_STEP * RECOVERY * UNIT_U / (UNIT_V * RATE)

P1 = MICRO_COUNT
P2 = P1 * MIDDLE
P3 = P2 * TOP
STEPS = P3 * OUTER
RING = MIDDLE + 1
SUB = 8
LANE = 128


def up(value, unit):
    return -(-value // unit) * unit


class Layout:
    def __init__(self, rows, cols, height, width):
        self.rows, self.cols = rows, cols
        self.height, self.width = height, width
        self.lanes = rows * height
        self.chunk = width // rows
        self.half = self.chunk // 2
        self.reach = up(STEPS, SUB)
        self.paired = rows & (rows - 1) == 0
        assert width % rows == 0 and self.chunk % LANE == 0
        assert height % SUB == 0 and self.chunk >= self.reach
        self.rank = [self._rank(i) for i in range(rows)]

    def _rank(self, i):
        if not self.paired:
            return i
        rank = 0
        while i:
            rank ^= i
            i >>= 1
        return rank

    def place(self, i, c):
        if isinstance(i, int):
            rank = self.rank[i]
        else:
            rank = sum(jnp.where(i == k, r, 0) for k, r in enumerate(self.rank))
        return rank + (c % 2) * (self.rows - 1 - 2 * rank)

    def target(self, i, d):
        return i ^ d if self.paired else (i + d) % self.rows

    def source(self, i, d):
        return i ^ d if self.paired else (i + self.rows - d) % self.rows

    def to_rows(self, d):
        return [(i, self.target(i, d)) for i in range(self.rows)]

    def ring(self, shift):
        line = {}
        for c in range(self.cols):
            for i in range(self.rows):
                line[c * self.rows + self.place(i, c)] = i * self.cols + c
        count = len(line)
        return [(line[q], line[(q + shift) % count]) for q in range(count)]

    def inner(self, t):
        return range(0, max(0, -(-(self.half - t) // SUB)))

    def low(self, t):
        return max(0, (self.half - t) // SUB)

    def outer(self, t):
        return range(self.low(t), -(-(self.half + self.reach - t) // SUB))

    def handed(self):
        have = {0: self.low(0)}
        need = []

        def want(time, block):
            for b in range(block, have[time]):
                need.append((time, b))
            have[time] = min(have[time], block)

        for t in range(1, STEPS + 1):
            low = self.low(t)
            want(t - 1, low)
            if t % P2 == 0:
                want(t - P1, low)
            if t % P3 == 0:
                want(t - P2, low)
            have[t] = low
        return sorted(need)


def even_lane(shape):
    return lax.broadcasted_iota(jnp.int32, shape, 1) % 2 == 0


def here():
    return lax.axis_index("row"), lax.axis_index("col")


def columns(lay, i, c):
    return pl.ds(pl.multiple_of(lay.place(i, c) * lay.chunk, LANE), lay.chunk)


def rows_of(lay, i):
    return pl.ds(pl.multiple_of(i * lay.height, SUB), lay.height)


def reverse_lanes(x):
    index = LANE - 1 - lax.broadcasted_iota(jnp.int32, x.shape, 1)
    return jnp.take_along_axis(x, index, axis=1)


def pack_kernel(lay, u, v, s, *refs):
    outs, ready = refs[: lay.rows], refs[lay.rows]
    i, c = here()
    copies = []
    for d in range(lay.rows):
        for f, field in enumerate((u, v, s)):
            part = field.at[:, columns(lay, lay.target(i, d), c)]
            copies.append(pltpu.make_async_copy(part, outs[d].at[f], ready.at[3 * d + f]))
    for copy in copies:
        copy.start()
    for copy in copies:
        copy.wait()


def interleave(lay, left, right):
    even = even_lane(left.shape)
    n = lay.lanes
    return (
        jnp.where(even, left, pltpu.roll(right, 1, 1)),
        jnp.where(even, pltpu.roll(left, n - 1, 1), right),
    )


def turn_kernel(lay, *refs):
    moved = refs[: lay.rows]
    state, drive, first, last, board = refs[lay.rows :]
    i, _ = here()
    tiles = lay.chunk // LANE
    for f in range(3):
        for d in range(lay.rows):
            board[f, rows_of(lay, lay.source(i, d)), :] = moved[d][f]
    for f in range(3):
        shift, scale = ((0.0, 1.0 / UNIT_U), (CENTRE, 1.0 / UNIT_V), (CENTRE, 1.0 / UNIT_V))[f]
        parts = [(board[f, :, a * LANE : (a + 1) * LANE] - shift) * scale for a in range(tiles)]
        ahead = jnp.concatenate([x.T for x in parts], axis=0)
        back = jnp.concatenate([reverse_lanes(x).T for x in reversed(parts)], axis=0)
        first[f] = ahead[: lay.reach]
        last[f] = back[: lay.reach]
        zero, one = interleave(lay, back[lay.half :], ahead[lay.half :])
        if f < 2:
            state[2 * f] = zero
            state[2 * f + 1] = one
        else:
            drive[0] = zero
            drive[1] = one


class Stage:
    def __init__(self, lay, kept, micro, offset, drive):
        self.lay, self.kept, self.micro, self.offset, self.drive = lay, kept, micro, offset, drive

    def at(self, t):
        if t % P1:
            return self.micro.at[t % P1 - 1]
        return self.kept.at[t // P1 % RING]

    def block(self, b):
        return pl.ds(self.offset + SUB * b, SUB)

    def line(self, x):
        return pl.ds(self.offset + x, 1)

    def fold(self, t, part, y):
        n = self.lay.lanes
        swapped = jnp.where(even_lane(y.shape), pltpu.roll(y, n - 1, 1), pltpu.roll(y, 1, 1))
        self.at(t)[part, self.line(-1), :] = swapped[0:1]

    def step(self, t, blocks):
        n = self.lay.lanes
        src, dst = self.at(t - 1), self.at(t)
        jump = t % P1 == 0
        second = t % P2 == 0
        third = t % P3 == 0
        scale = RATE * (2 if jump else 1) * (2 if second else 1) * (2 if third else 1)
        less = 0.5 / RATE if jump else 0.0
        for b in blocks:
            r = self.offset + SUB * b
            centre = [src[p, pl.ds(r, SUB), :] for p in range(4)]
            beside = [src[p, pl.ds(r - 1, SUB), :] + src[p, pl.ds(r + 1, SUB), :] for p in range(4)]
            for k in range(2):
                u, v = centre[k], centre[2 + k]
                other_u, other_v = centre[1 - k], centre[3 - k]
                turn = (2, n - 2)[k]
                near_u = beside[k] + (other_u + pltpu.roll(other_u, turn, 1))
                near_v = beside[2 + k] + (other_v + pltpu.roll(other_v, turn, 1))
                next_u = near_u + u * (KEEP_U - less - u * u) + (self.drive(k, b) - v)
                next_v = near_v + (v * (KEEP_V - less) + u * FEED)
                for part, y in ((k, next_u), (2 + k, next_v)):
                    if scale != 1.0:
                        y = y * scale
                    if second:
                        old = self.at(t - P1)[part, pl.ds(r, SUB), :]
                        if third:
                            old = old + old + self.at(t - P2)[part, pl.ds(r, SUB), :]
                        y = y - old
                    dst[part, pl.ds(r, SUB), :] = y
                    if b == 0:
                        self.fold(t, part, y)


def inner_kernel(lay, state, drive, lines, blocks, done, kept, micro):
    stage = Stage(lay, kept, micro, SUB, lambda k, b: drive[k, pl.ds(SUB * b, SUB), :])
    handed = lay.handed()
    for part in range(4):
        kept[0, part, SUB : SUB + lay.half, :] = state[part]
        stage.fold(0, part, state[part, 0:SUB, :])
    for t in range(STEPS + 1):
        if t:
            stage.step(t, lay.inner(t))
        if t == STEPS:
            break
        now = stage.at(t)
        low = lay.low(t + 1)
        for part in range(4):
            if low:
                lines[part, t : t + 1, :] = now[part, stage.line(SUB * low - 1), :]
            for j, (time, b) in enumerate(handed):
                if time == t:
                    blocks[part, SUB * j : SUB * j + SUB, :] = now[part, stage.block(b), :]
    final = lay.low(STEPS) * SUB
    if final:
        for part in range(4):
            done[part, 0:final, :] = stage.at(STEPS)[part, SUB : SUB + final, :]


def outer_kernel(lay, drive, lines, blocks, done, left, right, *refs):
    outs, (kept, micro, halo, board) = refs[: lay.rows], refs[lay.rows :]
    i, c = here()
    half, n = lay.half, lay.lanes

    def push(k, b):
        if SUB * b < half:
            return drive[k, pl.ds(SUB * b, SUB), :]
        return halo[k, pl.ds(SUB * b - half, SUB), :]

    base = SUB * lay.low(STEPS) - SUB
    stage = Stage(lay, kept, micro, -base, push)
    handed = lay.handed()
    for f in range(3):
        pair = interleave(lay, left[f], right[f])
        for k in range(2):
            if f < 2:
                kept[0, 2 * f + k, half - base : half - base + lay.reach, :] = pair[k]
            else:
                halo[k] = pair[k]
    for t in range(STEPS + 1):
        if t:
            stage.step(t, lay.outer(t))
        if t == STEPS:
            break
        now = stage.at(t)
        low = lay.low(t + 1)
        for part in range(4):
            if low:
                now[part, stage.line(SUB * low - 1), :] = lines[part, t : t + 1, :]
            for j, (time, b) in enumerate(handed):
                if time == t:
                    now[part, stage.block(b), :] = blocks[part, SUB * j : SUB * j + SUB, :]
                    if b == 0:
                        stage.fold(t, part, blocks[part, SUB * j : SUB * j + SUB, :])
    final = lay.low(STEPS) * SUB
    tiles = lay.chunk // LANE
    for f in range(2):
        pair = []
        for k in range(2):
            y = stage.at(STEPS)[2 * f + k, final - base : half - base, :]
            if final:
                y = jnp.concatenate([done[2 * f + k, 0:final, :], y], axis=0)
            pair.append(y * UNIT_V + CENTRE if f else y * UNIT_U)
        even = even_lane(pair[0].shape)
        west = jnp.where(even, pair[0], pltpu.roll(pair[1], 1, 1))
        east = jnp.where(even, pltpu.roll(pair[0], n - 1, 1), pair[1])
        if half % LANE:
            west, east = (jnp.concatenate([z[: LANE - half % LANE], z], axis=0) for z in (west, east))
        for a in range(tiles):
            lo, hi = a * LANE, (a + 1) * LANE
            skip = lay.chunk - east.shape[0]
            natural = reverse = None
            if hi > half:
                natural = east[lo - skip : hi - skip].T
            if lo < half:
                back = (tiles - 1 - a) * LANE - skip
                reverse = reverse_lanes(west[back : back + LANE].T)
            if natural is None:
                tile = reverse
            elif reverse is None:
                tile = natural
            else:
                lane = lax.broadcasted_iota(jnp.int32, natural.shape, 1)
                tile = jnp.where(lane < half - lo, reverse, natural)
            board[f, :, lo:hi] = tile
        for d in range(lay.rows):
            outs[d][f] = board[f, rows_of(lay, lay.target(i, d)), :]


def place_kernel(lay, *refs):
    pieces, (u, v) = refs[: lay.rows], refs[lay.rows :]
    i, c = here()
    for d in range(lay.rows):
        for f, out in enumerate((u, v)):
            out[:, columns(lay, lay.source(i, d), c)] = pieces[d][f]


def shape(*dims):
    return jax.ShapeDtypeStruct(dims, jnp.float32)


def call(kernel, lay, outs, scratch, name, mib, **specs):
    return pl.pallas_call(
        functools.partial(kernel, lay),
        out_shape=outs,
        **specs,
        scratch_shapes=[pltpu.VMEM(x, jnp.float32) if isinstance(x, tuple) else x for x in scratch],
        compiler_params=pltpu.CompilerParams(vmem_limit_bytes=mib * 2**20),
        name=name,
    )


def body(lay, u_field, v_field, stimulus):
    r, h, w, n = lay.rows, lay.height, lay.chunk, lay.lanes
    half, reach = lay.half, lay.reach
    fields = (u_field, v_field, stimulus)
    packs = call(
        pack_kernel,
        lay,
        [shape(3, h, w)] * r,
        [pltpu.SemaphoreType.DMA((3 * r,))],
        "pack",
        8,
        in_specs=[pl.BlockSpec(memory_space=pltpu.HBM)] * 3,
    )(*fields)
    moved = [packs[0]] + [lax.ppermute(packs[d], "row", lay.to_rows(d)) for d in range(1, r)]
    state, drive, first, last = call(
        turn_kernel,
        lay,
        [shape(4, half, n), shape(2, half, n), shape(3, reach, n), shape(3, reach, n)],
        [(3, n, w)],
        "turn",
        8,
    )(*moved)
    right = lax.ppermute(first, ("row", "col"), lay.ring(-1))
    left = lax.ppermute(last, ("row", "col"), lay.ring(1))
    extra = max(1, len(lay.handed()))
    final = max(1, lay.low(STEPS))
    lines, blocks, done = call(
        inner_kernel,
        lay,
        [shape(4, reach, n), shape(4, SUB * extra, n), shape(4, SUB * final, n)],
        [(RING, 4, half + 2 * SUB, n), (P1 - 1, 4, half + 2 * SUB, n)],
        "inner",
        16,
    )(state, drive)
    span = half + reach + 2 * SUB - SUB * lay.low(STEPS)
    pieces = call(
        outer_kernel,
        lay,
        [shape(2, h, w)] * r,
        [(RING, 4, span, n), (P1 - 1, 4, span, n), (2, reach, n), (2, n, w)],
        "outer",
        24,
    )(drive, lines, blocks, done, left, right)
    back = [pieces[0]] + [lax.ppermute(pieces[d], "row", lay.to_rows(d)) for d in range(1, r)]
    return tuple(
        call(place_kernel, lay, [shape(h, lay.width)] * 2, [], "place", 8)(*back)
    )


def solution(mesh):
    def run(u_field, v_field, stimulus):
        lay = Layout(mesh.shape["row"], mesh.shape["col"], *u_field.shape)
        return body(lay, u_field, v_field, stimulus)

    return jax.shard_map(
        run,
        mesh=mesh,
        in_specs=(P("row", "col"),) * 3,
        out_specs=(P("row", "col"),) * 2,
        check_vma=False,
    )
```

time: 174 us -> 39.5 us (0.23)
  other arithmetic: 73.5 us -> 0 us
  waiting for transfers between devices: 46.6 us -> 7.74 us
  starting transfers between devices: 40.1 us -> 11.7 us
  Pallas kernels: 0 us -> 16.5 us
  local copies, waits for them, and re-layouts: 11.3 us -> 2.7 us
    ppermute x28 -> x8, waiting for transfers between devices: 46.6 us -> 7.74 us  [the longest x3 5.49 us: body(): lax.ppermute(packs[d], 'row', lay.to_rows(d))]
    sub x72 -> x0, other arithmetic: 36.3 us -> none  [advance(): beside_all = beside_all - 4.0 * centre]
    ppermute x28 -> x8, starting transfers between devices: 40.1 us -> 11.7 us  [the longest x3 4.57 us: body(): lax.ppermute(packs[d], 'row', lay.to_rows(d))]
    add x92 -> x0, other arithmetic: 20 us -> none  [the longest x66 12.3 us: advance(): v_now + RATE_V * beside_all[1]]
    another operation x67 -> x0, other arithmetic: 16.9 us -> none  [the longest x66 16.2 us: advance(): return jnp.stack([u_next, v_next])]
    pallas_call x0 -> x5, Pallas kernels: none -> 16.5 us  [the longest x1 7.72 us: body(): call(outer_kernel, lay, [shape(2, h, w)] * r, [(RING, 4, span, n), (P1 -...]
    while x8 -> x0, local copies, waits for them, and re-layouts: 6.04 us -> none
    unnamed x8 -> x6, local copies, waits for them, and re-layouts: 0.02 us -> 2.7 us
  transfers between devices with their start and end apart: 28 -> 8, of which waited for: 22 -> 6; matrix products, arithmetic and copies ran while one was open for 3% -> 0% of each run, Pallas kernels for 0% -> 18%
where the time goes in v1:
time: 39.5 us; the launch traced here: 39.4 us
  Pallas kernels  16.5 us (42%)
  starting transfers between devices  11.7 us (30%)
  waiting for transfers between devices  7.74 us (20%)
  local copies, waits for them, and re-layouts  2.7 us (7%)
  between operations  0.7 us (2%)
    pallas_call x1, Pallas kernels, body(): call(outer_kernel, lay, [shape(2, h, w)] * r, [(RING, 4, span, n), (P1 -...  7.72 us
    pallas_call x1, Pallas kernels, body(): call(inner_kernel, lay, [shape(4, reach, n), shape(4, SUB * extra, n), sh...  7.03 us
    ppermute x3, waiting for transfers between devices, body(): lax.ppermute(packs[d], 'row', lay.to_rows(d))  5.49 us
    ppermute x3, starting transfers between devices, body(): lax.ppermute(packs[d], 'row', lay.to_rows(d))  4.57 us
    ppermute x3, starting transfers between devices, body(): lax.ppermute(pieces[d], 'row', lay.to_rows(d))  3.54 us
    ppermute x1, starting transfers between devices, body(): right = lax.ppermute(first, ('row', 'col'), lay.ring(-1))  2.9 us
    unnamed x6, local copies, waits for them, and re-layouts  2.7 us
    ppermute x3, waiting for transfers between devices, body(): lax.ppermute(pieces[d], 'row', lay.to_rows(d))  2.24 us
  transfers between devices with their start and end apart: 8, of which 6 were waited for; matrix products, arithmetic and copies ran while one was open for 0% of the time, Pallas kernels for 18%

profile of v1, /device:TPU:0, one launch (start us, length us, event | category | flops | bytes accessed | tf_op | source)
XLA Modules:
  0.0 39.4 jit_solution(17627135532602525152)
XLA Ops:
  0.6 0.0 copy-start
  0.6 0.9 %copy-done = f32[32,1024]{1,0:T(8,128)S(1)} copy-done((f32[32,1024]{1,0:T(8,128)S(1)}, f32[32,1024]{1,0:T(8,128)}, u32[]{:S(2)}) %copy-start) | copy-done | bytes 131096
  1.5 0.0 copy-start.1
  1.5 0.9 %copy-done.1 = f32[32,1024]{1,0:T(8,128)S(1)} copy-done((f32[32,1024]{1,0:T(8,128)S(1)}, f32[32,1024]{1,0:T(8,128)}, u32[]{:S(2)}) %copy-start.1) | copy-done | bytes 131096
  2.4 0.0 copy-start.2
  2.4 0.9 %copy-done.2 = f32[32,1024]{1,0:T(8,128)S(1)} copy-done((f32[32,1024]{1,0:T(8,128)S(1)}, f32[32,1024]{1,0:T(8,128)}, u32[]{:S(2)}) %copy-start.2) | copy-done | bytes 131096
  3.3 0.2 pack.1
  3.6 3.0 %collective-permute-start = (f32[3,32,256]{2,1,0:T(8,128)S(1)}, f32[3,32,256]{2,1,0:T(8,128)S(1)}, u32[]{:S(2)}, u32[]{:S(2)}) collective-permute-start(f32[3,32,256]{2,1,0:T(8,128)S(1)} %get-tuple-element.18), channel_id=1, source_target_pairs={{0,8},{8,0},{16,24},{24,16},{1,9},{9,1},{17,25},{25,17},{2,10},{10... | collective-permute-start | bytes 294920 | tf_op jit(solution)/shard_map/ppermute | solution.py:368
  6.6 1.5 %collective-permute-start.1 = (f32[3,32,256]{2,1,0:T(8,128)S(1)}, f32[3,32,256]{2,1,0:T(8,128)S(1)}, u32[]{:S(2)}, u32[]{:S(2)}) collective-permute-start(f32[3,32,256]{2,1,0:T(8,128)S(1)} %get-tuple-element.19), channel_id=1, source_target_pairs={{0,16},{8,24},{16,0},{24,8},{1,17},{9,25},{17,1},{25,9},{2,18},{10... | collective-permute-start | bytes 294920 | tf_op jit(solution)/shard_map/ppermute | solution.py:368
  8.2 0.0 collective-permute-start.2
  8.2 1.5 %collective-permute-done.refs_1_ = f32[3,32,256]{2,1,0:T(8,128)S(1)} collective-permute-done((f32[3,32,256]{2,1,0:T(8,128)S(1)}, f32[3,32,256]{2,1,0:T(8,128)S(1)}, u32[]{:S(2)}, u32[]{:S(2)}) %collective-permute-start) | collective-permute-done | bytes 98336 | tf_op jit(solution)/shard_map/ppermute | solution.py:368
  9.7 2.6 %collective-permute-done.1.refs_2_ = f32[3,32,256]{2,1,0:T(8,128)S(1)} collective-permute-done((f32[3,32,256]{2,1,0:T(8,128)S(1)}, f32[3,32,256]{2,1,0:T(8,128)S(1)}, u32[]{:S(2)}, u32[]{:S(2)}) %collective-permute-start.1) | collective-permute-done | bytes 98336 | tf_op jit(solution)/shard_map/ppermute | solution.py:368
  12.3 1.4 %collective-permute-done.2.refs_3_ = f32[3,32,256]{2,1,0:T(8,128)S(1)} collective-permute-done((f32[3,32,256]{2,1,0:T(8,128)S(1)}, f32[3,32,256]{2,1,0:T(8,128)S(1)}, u32[]{:S(2)}, u32[]{:S(2)}) %collective-permute-start.2) | collective-permute-done | bytes 98336 | tf_op jit(solution)/shard_map/ppermute | solution.py:368
  13.7 0.8 %turn.1 = (f32[4,128,128]{2,1,0:T(8,128)S(1)}, f32[2,128,128]{2,1,0:T(8,128)S(1)}, f32[3,72,128]{2,1,0:T(8,128)S(1)}, f32[3,72,128]{2,1,0:T(8,128)S(1)}) custom-call(f32[3,32,256]{2,1,0:T(8,128)S(1)} %get-tuple-element.17.refs_0_, f32[3,32,256]{2,1,0:T(8,128)S(1)} %collective-permute-done.refs_1_, f32[3,32,256]{2,1,0:T(8,128)S(1)} %collective-permute-done.1.refs_2_, ...), custom_call_target="tpu_custom_call" | custom-call | tf_op jit(solution)/shard_map/turn/pallas_call | solution.py:369
  14.4 0.7 %collective-permute-start.3 = (f32[3,72,128]{2,1,0:T(8,128)S(1)}, f32[3,72,128]{2,1,0:T(8,128)S(1)}, u32[]{:S(2)}, u32[]{:S(2)}) collective-permute-start(f32[3,72,128]{2,1,0:T(8,128)S(1)} %get-tuple-element.26), channel_id=1, source_target_pairs={{0,8},{8,24},{24,16},{16,17},{17,25},{25,9},{9,1},{1,2},{2,10},{10... | collective-permute-start | bytes 331784 | tf_op jit(solution)/shard_map/ppermute | solution.py:378
  15.1 2.9 %collective-permute-start.4 = (f32[3,72,128]{2,1,0:T(8,128)S(1)}, f32[3,72,128]{2,1,0:T(8,128)S(1)}, u32[]{:S(2)}, u32[]{:S(2)}) collective-permute-start(f32[3,72,128]{2,1,0:T(8,128)S(1)} %get-tuple-element.27), channel_id=1, source_target_pairs={{0,7},{8,0},{24,8},{16,24},{17,16},{25,17},{9,25},{1,9},{2,1},{10,... | collective-permute-start | bytes 331784 | tf_op jit(solution)/shard_map/ppermute | solution.py:377
  18.0 7.0 %inner.1 = (f32[4,72,128]{2,1,0:T(8,128)S(1)}, f32[4,88,128]{2,1,0:T(8,128)S(1)}, f32[4,56,128]{2,1,0:T(8,128)S(1)}) custom-call(f32[4,128,128]{2,1,0:T(8,128)S(1)} %get-tuple-element.22.state, f32[2,128,128]{2,1,0:T(8,128)S(1)} %get-tuple-element.21.drive), custom_call_target="tpu_custom_call" | custom-call | tf_op jit(solution)/shard_map/inner/pallas_call | solution.py:381
  25.1 0.0 collective-permute-done.3.left
  25.1 0.0 collective-permute-done.4.right
  25.1 7.7 %outer.1 = (f32[2,32,256]{2,1,0:T(8,128)S(1)}, f32[2,32,256]{2,1,0:T(8,128)S(1)}, f32[2,32,256]{2,1,0:T(8,128)S(1)}, f32[2,32,256]{2,1,0:T(8,128)S(1)}) custom-call(f32[2,128,128]{2,1,0:T(8,128)S(1)} %get-tuple-element.21.drive, f32[4,72,128]{2,1,0:T(8,128)S(1)} %get-tuple-element.23.lines, f32[4,88,128]{2,1,0:T(8,128)S(1)} %get-tuple-element.24.blocks, ...), custom_call_target="tpu_custom_call" | custom-call | tf_op jit(solution)/shard_map/outer/pallas_call | solution.py:390
  32.8 0.1 collective-permute-start.5
  32.9 0.1 collective-permute-start.6
  33.0 3.4 %collective-permute-start.7 = (f32[2,32,256]{2,1,0:T(8,128)S(1)}, f32[2,32,256]{2,1,0:T(8,128)S(1)}, u32[]{:S(2)}, u32[]{:S(2)}) collective-permute-start(f32[2,32,256]{2,1,0:T(8,128)S(1)} %get-tuple-element.31), channel_id=1, source_target_pairs={{0,24},{8,16},{16,8},{24,0},{1,25},{9,17},{17,9},{25,1},{2,26},{10... | collective-permute-start | bytes 196616 | tf_op jit(solution)/shard_map/ppermute | solution.py:398
  36.4 0.8 %collective-permute-done.5.refs_1_ = f32[2,32,256]{2,1,0:T(8,128)S(1)} collective-permute-done((f32[2,32,256]{2,1,0:T(8,128)S(1)}, f32[2,32,256]{2,1,0:T(8,128)S(1)}, u32[]{:S(2)}, u32[]{:S(2)}) %collective-permute-start.5) | collective-permute-done | bytes 65568 | tf_op jit(solution)/shard_map/ppermute | solution.py:398
  37.2 0.1 collective-permute-done.6.refs_2_
  37.2 1.4 %collective-permute-done.7.refs_3_ = f32[2,32,256]{2,1,0:T(8,128)S(1)} collective-permute-done((f32[2,32,256]{2,1,0:T(8,128)S(1)}, f32[2,32,256]{2,1,0:T(8,128)S(1)}, u32[]{:S(2)}, u32[]{:S(2)}) %collective-permute-start.7) | collective-permute-done | bytes 65568 | tf_op jit(solution)/shard_map/ppermute | solution.py:398
  38.6 0.7 %place.1 = (f32[32,1024]{1,0:T(8,128)}, f32[32,1024]{1,0:T(8,128)}) custom-call(f32[2,32,256]{2,1,0:T(8,128)S(1)} %get-tuple-element.28.refs_0_, f32[2,32,256]{2,1,0:T(8,128)S(1)} %collective-permute-done.5.refs_1_, f32[2,32,256]{2,1,0:T(8,128)S(1)} %collective-permute-done.6.refs_2_, f32[2,32,256]{2,1,0:T(8,128)S(1)} %collective-permute-done.7.refs_3_), custom_call_target="tpu_custom_call" | custom-call | tf_op jit(solution)/shard_map/place/pallas_call | solution.py:400
Async XLA Ops:
  0.6 0.9 %copy-start = (f32[32,1024]{1,0:T(8,128)S(1)}, f32[32,1024]{1,0:T(8,128)}, u32[]{:S(2)}) copy-start(f32[32,1024]{1,0:T(8,128)} %u.1) | copy-start | bytes 393220
  1.5 0.9 %copy-start.1 = (f32[32,1024]{1,0:T(8,128)S(1)}, f32[32,1024]{1,0:T(8,128)}, u32[]{:S(2)}) copy-start(f32[32,1024]{1,0:T(8,128)} %v.1) | copy-start | bytes 393220
  2.4 0.9 %copy-start.2 = (f32[32,1024]{1,0:T(8,128)S(1)}, f32[32,1024]{1,0:T(8,128)}, u32[]{:S(2)}) copy-start(f32[32,1024]{1,0:T(8,128)} %s.1) | copy-start | bytes 393220
  3.6 6.1 %collective-permute-start = (f32[3,32,256]{2,1,0:T(8,128)S(1)}, f32[3,32,256]{2,1,0:T(8,128)S(1)}, u32[]{:S(2)}, u32[]{:S(2)}) collective-permute-start(f32[3,32,256]{2,1,0:T(8,128)S(1)} %get-tuple-element.18), channel_id=1, source_target_pairs={{0,8},{8,0},{16,24},{24,16},{1,9},{9,1},{17,25},{25,17},{2,10},{10... | collective-permute-start | bytes 294920 | tf_op jit(solution)/shard_map/ppermute | solution.py:368
  6.6 5.7 %collective-permute-start.1 = (f32[3,32,256]{2,1,0:T(8,128)S(1)}, f32[3,32,256]{2,1,0:T(8,128)S(1)}, u32[]{:S(2)}, u32[]{:S(2)}) collective-permute-start(f32[3,32,256]{2,1,0:T(8,128)S(1)} %get-tuple-element.19), channel_id=1, source_target_pairs={{0,16},{8,24},{16,0},{24,8},{1,17},{9,25},{17,1},{25,9},{2,18},{10... | collective-permute-start | bytes 294920 | tf_op jit(solution)/shard_map/ppermute | solution.py:368
  8.2 5.5 %collective-permute-start.2 = (f32[3,32,256]{2,1,0:T(8,128)S(1)}, f32[3,32,256]{2,1,0:T(8,128)S(1)}, u32[]{:S(2)}, u32[]{:S(2)}) collective-permute-start(f32[3,32,256]{2,1,0:T(8,128)S(1)} %get-tuple-element.20), channel_id=1, source_target_pairs={{0,24},{8,16},{16,8},{24,0},{1,25},{9,17},{17,9},{25,1},{2,26},{10... | collective-permute-start | bytes 294920 | tf_op jit(solution)/shard_map/ppermute | solution.py:368
  14.4 10.6 %collective-permute-start.3 = (f32[3,72,128]{2,1,0:T(8,128)S(1)}, f32[3,72,128]{2,1,0:T(8,128)S(1)}, u32[]{:S(2)}, u32[]{:S(2)}) collective-permute-start(f32[3,72,128]{2,1,0:T(8,128)S(1)} %get-tuple-element.26), channel_id=1, source_target_pairs={{0,8},{8,24},{24,16},{16,17},{17,25},{25,9},{9,1},{1,2},{2,10},{10... | collective-permute-start | bytes 331784 | tf_op jit(solution)/shard_map/ppermute | solution.py:378
  15.1 9.9 %collective-permute-start.4 = (f32[3,72,128]{2,1,0:T(8,128)S(1)}, f32[3,72,128]{2,1,0:T(8,128)S(1)}, u32[]{:S(2)}, u32[]{:S(2)}) collective-permute-start(f32[3,72,128]{2,1,0:T(8,128)S(1)} %get-tuple-element.27), channel_id=1, source_target_pairs={{0,7},{8,0},{24,8},{16,24},{17,16},{25,17},{9,25},{1,9},{2,1},{10,... | collective-permute-start | bytes 331784 | tf_op jit(solution)/shard_map/ppermute | solution.py:377
  32.8 4.3 %collective-permute-start.5 = (f32[2,32,256]{2,1,0:T(8,128)S(1)}, f32[2,32,256]{2,1,0:T(8,128)S(1)}, u32[]{:S(2)}, u32[]{:S(2)}) collective-permute-start(f32[2,32,256]{2,1,0:T(8,128)S(1)} %get-tuple-element.29), channel_id=1, source_target_pairs={{0,8},{8,0},{16,24},{24,16},{1,9},{9,1},{17,25},{25,17},{2,10},{10... | collective-permute-start | bytes 196616 | tf_op jit(solution)/shard_map/ppermute | solution.py:398
  32.9 4.3 %collective-permute-start.6 = (f32[2,32,256]{2,1,0:T(8,128)S(1)}, f32[2,32,256]{2,1,0:T(8,128)S(1)}, u32[]{:S(2)}, u32[]{:S(2)}) collective-permute-start(f32[2,32,256]{2,1,0:T(8,128)S(1)} %get-tuple-element.30), channel_id=1, source_target_pairs={{0,16},{8,24},{16,0},{24,8},{1,17},{9,25},{17,1},{25,9},{2,18},{10... | collective-permute-start | bytes 196616 | tf_op jit(solution)/shard_map/ppermute | solution.py:398
  33.0 5.6 %collective-permute-start.7 = (f32[2,32,256]{2,1,0:T(8,128)S(1)}, f32[2,32,256]{2,1,0:T(8,128)S(1)}, u32[]{:S(2)}, u32[]{:S(2)}) collective-permute-start(f32[2,32,256]{2,1,0:T(8,128)S(1)} %get-tuple-element.31), channel_id=1, source_target_pairs={{0,24},{8,16},{16,8},{24,0},{1,25},{9,17},{17,9},{25,1},{2,26},{10... | collective-permute-start | bytes 196616 | tf_op jit(solution)/shard_map/ppermute | solution.py:398
